TPU v7x, 32 devices: a whole 2x2x4 slice. The times are simulated.
32 devices in a mesh: fsdp: 16 (over z, y, x), tp: 2 (over core).
Axes of the slice: x: 2, y: 2, z: 4, core: 2. Of those that a mesh axis runs over, the one named last changes fastest.
Arguments:
- owner: int32 [2, 7], replicated, may hold values from 0 to 15, as said below
- grads: bfloat16 [2, 896, 2, 8320], P(None, 'fsdp', 'tp')
- weights: float32 [2, 896, 2, 8320], P(None, 'fsdp', 'tp'), may hold values from -0.1875 to 0.1875
- adam_m: float32 [2, 896, 2, 8320], P(None, 'fsdp', 'tp'), may hold values from -0.4375 to 0.4375
- adam_v: float32 [2, 896, 2, 8320], P(None, 'fsdp', 'tp'), may hold values from 0.0001 to 0.1
- stats: float32 [16, 896, 896], P('fsdp', 'tp')
- roots: bfloat16 [16, 896, 896], P('fsdp', 'tp')
- vec_weight: float32 [2, 2944], P(None, ('fsdp', 'tp')), may hold values from 0.5 to 1.5
- vec_grad: bfloat16 [2, 2944], P(None, ('fsdp', 'tp')), may hold values from -1.5 to 1.5
- vec_m: float32 [2, 2944], P(None, ('fsdp', 'tp')), may hold values from -0.4375 to 0.4375
- vec_v: float32 [2, 2944], P(None, ('fsdp', 'tp')), may hold values from 0.0001 to 0.1
Outputs:
- weights_new: float32 [2, 896, 2, 8320], P(None, 'fsdp', 'tp')
- adam_m_new: float32 [2, 896, 2, 8320], P(None, 'fsdp', 'tp')
- adam_v_new: float32 [2, 896, 2, 8320], P(None, 'fsdp', 'tp')
- stats_new: float32 [16, 896, 896], P('fsdp', 'tp')
- vec_weight_new: float32 [2, 2944], P(None, ('fsdp', 'tp'))
- vec_m_new: float32 [2, 2944], P(None, ('fsdp', 'tp'))
- vec_v_new: float32 [2, 2944], P(None, ('fsdp', 'tp'))
Inputs may be any that keep to these rules, and one draw needn't show every extreme that they name: owner[l, t] is the index along fsdp of the chip whose slot holds the statistic of kind t of layer l; all 14 values are distinct, so a chip owns at most one matrix and some chips own none.
All inputs are finite; a program needn't handle non-finite values.
Results may differ from a plain program's by a relative error of at most 0.0015.
Values may be sent and summed in bfloat16 or wider, within the bound.
No kernel may reach another device: no remote copies, remote signals or barrier semaphores. Data moves between devices by JAX's collectives and lax.ppermute only.
A program may use at most 192 MiB of HBM per device.

v0:
```python
import jax
import jax.numpy as jnp
from jax import lax
from jax.sharding import PartitionSpec as P

FF = 4864
QW = 896
KW = 128


def half_widths():
    return [QW // 2, KW // 2, KW // 2, QW // 2, FF // 2, FF // 2, FF // 2]


def column_starts(widths):
    starts = []
    position = 0
    for wide in widths:
        starts.append(position)
        position = position + wide
    return starts


def kind_sums(values, widths, starts):
    return jnp.stack(
        [
            jnp.sum(values[:, :, starts[kind] : starts[kind] + widths[kind]], axis=(1, 2))
            for kind in range(7)
        ],
        axis=1,
    )


def gram_rows(left, right):
    return lax.dot_general(
        left, right, (((1,), (1,)), ((), ())), preferred_element_type=jnp.float32
    )


def on_device(
    owner, grads, weights, adam_m, adam_v, stats, roots, vec_weight, vec_grad, vec_m, vec_v
):
    widths = half_widths()
    starts = column_starts(widths)
    classes = [widths[0], widths[1], widths[4]]
    class_table = jnp.array([0, 1, 1, 0, 2, 2, 2], jnp.int32)
    chips = lax.axis_size("fsdp")
    layers = grads.shape[0]
    rows = grads.shape[1]
    capacity = FF // 2
    model_rows = rows * chips
    local_grad = grads[:, :, 0, :]
    grad_float = grads.astype(jnp.float32)
    adam_m_new = 0.9 * adam_m + 0.1 * grad_float
    adam_v_new = 0.99 * adam_v + 0.01 * grad_float * grad_float
    adam_step = (adam_m_new / (jnp.sqrt(adam_v_new) + 1e-08))[:, :, 0, :]
    adam_part = kind_sums(adam_step * adam_step, widths, starts)
    adam_total = lax.psum(adam_part, ("fsdp", "tp"))
    outgoing = jnp.zeros((chips, rows, capacity), jnp.bfloat16)
    for kind in range(7):
        outgoing = outgoing.at[owner[:, kind], :, : widths[kind]].set(
            local_grad[:, :, starts[kind] : starts[kind] + widths[kind]]
        )
    arrived = lax.all_to_all(outgoing, "fsdp", split_axis=0, concat_axis=0, tiled=True)
    gathered = arrived.reshape(model_rows, capacity)
    chip_index = lax.axis_index("fsdp")
    matches = owner == chip_index
    owned = jnp.any(matches)
    width_class = jnp.where(owned, jnp.sum(jnp.where(matches, class_table[None, :], 0)), 1)
    stat_slot = stats[0]
    root_slot = roots[0]

    def stat_term_rows():

        def make_rows(wide):

            def branch():
                block = gathered[:, :wide]
                return gram_rows(block, gathered[:, :wide])

            return branch

        return lax.switch(width_class, [make_rows(wide) for wide in classes])

    stat_term = lax.psum_scatter(stat_term_rows(), "tp", scatter_dimension=0, tiled=True)

    def apply_rows(piece):

        def make_apply(wide):

            def branch():
                result = jnp.dot(piece, gathered[:, :wide], preferred_element_type=jnp.float32)
                return jnp.pad(result, ((0, 0), (0, capacity - wide)))

            return branch

        return lax.switch(width_class, [make_apply(wide) for wide in classes])

    precond = apply_rows(lax.all_gather(root_slot, "tp", axis=0, tiled=True)).astype(jnp.bfloat16)
    stats_new = jnp.where(owned, 0.9 * stat_slot + 0.1 * stat_term, stat_slot)[None]
    returned = lax.all_to_all(
        precond.reshape(chips, rows, capacity), "fsdp", split_axis=0, concat_axis=0, tiled=True
    )
    pieces = [returned[owner[:, kind], :, : widths[kind]] for kind in range(7)]
    direction = jnp.concatenate(pieces, axis=2).astype(jnp.float32)
    shampoo_part = kind_sums(direction * direction, widths, starts)
    shampoo_total = lax.psum(shampoo_part, ("fsdp", "tp"))
    ratio = jnp.sqrt(adam_total) / (jnp.sqrt(shampoo_total) + 1e-06)
    column_scale = jnp.concatenate(
        [jnp.broadcast_to(ratio[:, kind : kind + 1], (layers, widths[kind])) for kind in range(7)],
        axis=1,
    )
    weights_new = weights - 0.02 * (direction * column_scale[:, None, :])[:, :, None, :]
    vec_float = vec_grad.astype(jnp.float32)
    vec_m_new = 0.9 * vec_m + 0.1 * vec_float
    vec_v_new = 0.99 * vec_v + 0.01 * vec_float * vec_float
    vec_weight_new = vec_weight - 0.02 * vec_m_new / (jnp.sqrt(vec_v_new) + 1e-08)
    return (weights_new, adam_m_new, adam_v_new, stats_new, vec_weight_new, vec_m_new, vec_v_new)


def solution(mesh):
    placed = (
        P(),
        P(None, "fsdp", "tp", None),
        P(None, "fsdp", "tp", None),
        P(None, "fsdp", "tp", None),
        P(None, "fsdp", "tp", None),
        P("fsdp", "tp", None),
        P("fsdp", "tp", None),
        P(None, ("fsdp", "tp")),
        P(None, ("fsdp", "tp")),
        P(None, ("fsdp", "tp")),
        P(None, ("fsdp", "tp")),
    )
    return jax.shard_map(
        on_device,
        mesh=mesh,
        in_specs=placed,
        out_specs=(
            P(None, "fsdp", "tp", None),
            P(None, "fsdp", "tp", None),
            P(None, "fsdp", "tp", None),
            P("fsdp", "tp", None),
            P(None, ("fsdp", "tp")),
            P(None, ("fsdp", "tp")),
            P(None, ("fsdp", "tp")),
        ),
        check_vma=False,
    )
```

profile of v0, /device:TPU:0, one launch (start us, length us, event | category | flops | bytes accessed | tf_op | source)
XLA Modules:
  0.0 411.3 jit_solution(16580479824753953919)
XLA Ops:
  8.0 1.1 fusion.25
  9.1 1.5 fusion.24
  11.0 2.3 broadcast_in_dim.46
  13.3 16.8 %while.4 = (s32[]{:T(128)}, bf16[16,56,2432]{2,1,0:T(8,128)(2,1)}, s32[2,2]{1,0:T(2,128)S(1)}, bf16[2,56,448]{2,1,0:T(8,128)(2,1)S(1)}, s32[]{:T(128)}, /*index=5*/s32[3]{0:T(128)S(1)}, s32[1]{0:T(128)}, s32[]{:T(128)}) while((s32[]{:T(128)}, bf16[16,56,2432]{2,1,0:T(8,128)(2,1)}, s32[2,2]{1,0:T(2,128)S(1)}, bf16[2,56,448]{2,1,0:T(8,128)(2,1)S(1)}, ...), condition=%wide.while_cond, body=%wide.while_body.sunk | while | flops 25107 | bytes 251051 | solution.py:61
  13.9 2.0 and_reduce_fusion.8
  15.9 2.9 dynamic-slice_select_fusion.8
  18.8 2.9 dynamic-update-slice.12
  22.3 2.0 and_reduce_fusion.8
  24.3 2.9 dynamic-slice_select_fusion.8
  27.2 2.9 dynamic-update-slice.12
  30.1 16.1 %while.5 = (s32[]{:T(128)}, bf16[16,56,2432]{2,1,0:T(8,128)(2,1)}, s32[2,2]{1,0:T(2,128)S(1)}, bf16[2,56,64]{2,1,0:T(8,128)(2,1)S(1)}, s32[]{:T(128)}, /*index=5*/s32[3]{0:T(128)S(1)}, s32[1]{0:T(128)}, s32[]{:T(128)}) while((s32[]{:T(128)}, bf16[16,56,2432]{2,1,0:T(8,128)(2,1)}, s32[2,2]{1,0:T(2,128)S(1)}, bf16[2,56,64]{2,1,0:T(8,128)(2,1)S(1)}, ...), condition=%wide.while_cond.1, body=%wide.while_body.1.sunk | while | flops 3603 | bytes 36011 | solution.py:61
  30.7 2.0 and_reduce_fusion.9
  32.7 2.8 dynamic-slice_select_fusion.9
  35.5 2.7 dynamic-update-slice.13
  38.7 2.0 and_reduce_fusion.9
  40.7 2.8 dynamic-slice_select_fusion.9
  43.5 2.7 dynamic-update-slice.13
  46.2 16.1 %while.6 = (s32[]{:T(128)}, bf16[16,56,2432]{2,1,0:T(8,128)(2,1)}, s32[2,2]{1,0:T(2,128)S(1)}, bf16[2,56,64]{2,1,0:T(8,128)(2,1)S(1)}, s32[]{:T(128)}, /*index=5*/s32[3]{0:T(128)S(1)}, s32[1]{0:T(128)}, s32[]{:T(128)}) while((s32[]{:T(128)}, bf16[16,56,2432]{2,1,0:T(8,128)(2,1)}, s32[2,2]{1,0:T(2,128)S(1)}, bf16[2,56,64]{2,1,0:T(8,128)(2,1)S(1)}, ...), condition=%wide.while_cond.2, body=%wide.while_body.2.sunk | while | flops 3603 | bytes 36011 | solution.py:61
  46.8 2.0 and_reduce_fusion.10
  48.8 2.8 dynamic-slice_select_fusion.10
  51.5 2.7 dynamic-update-slice.14
  54.8 2.0 and_reduce_fusion.10
  56.8 2.8 dynamic-slice_select_fusion.10
  59.6 2.7 dynamic-update-slice.14
  62.3 16.7 %while.7 = (s32[]{:T(128)}, bf16[16,56,2432]{2,1,0:T(8,128)(2,1)}, s32[2,2]{1,0:T(2,128)S(1)}, bf16[2,56,448]{2,1,0:T(8,128)(2,1)S(1)}, s32[]{:T(128)}, /*index=5*/s32[3]{0:T(128)S(1)}, s32[1]{0:T(128)}, s32[]{:T(128)}) while((s32[]{:T(128)}, bf16[16,56,2432]{2,1,0:T(8,128)(2,1)}, s32[2,2]{1,0:T(2,128)S(1)}, bf16[2,56,448]{2,1,0:T(8,128)(2,1)S(1)}, ...), condition=%wide.while_cond.3, body=%wide.while_body.3.sunk | while | flops 25107 | bytes 251051 | solution.py:61
  62.9 2.0 and_reduce_fusion.11
  64.9 2.9 dynamic-slice_select_fusion.11
  67.8 2.9 dynamic-update-slice.15
  71.2 2.0 and_reduce_fusion.11
  73.2 2.9 dynamic-slice_select_fusion.11
  76.2 2.9 dynamic-update-slice.15
  79.0 2.4 scatter_fusion
  81.5 2.4 scatter_fusion.1
  83.9 2.4 scatter_fusion.2
  86.3 8.5 %all-to-all-start = ((bf16[16,56,2432]{2,1,0:T(8,128)(2,1)}), bf16[16,56,2432]{2,1,0:T(8,128)(2,1)}, u32[]{:S(2)}, u32[]{:S(2)}) async-start(bf16[16,56,2432]{2,1,0:T(8,128)(2,1)} %scatter_fusion.2), calls=%async_computation | async-start | bytes 8716288 | tf_op jit(solution)/shard_map/all_to_all | solution.py:64
  98.0 10.3 %all-gather.3.cloned.1.call-done = bf16[1,896,896]{2,1,0:T(8,128)(2,1)} async-done(((bf16[1,448,896]{2,1,0:T(8,128)(2,1)}), bf16[1,896,896]{2,1,0:T(8,128)(2,1)}) %all-gather.3.cloned.1.call-update) | async-done | bytes 1605648 | tf_op jit(solution)/shard_map/all_gather | solution.py:99
  108.3 69.2 %all-to-all-done = bf16[16,56,2432]{2,1,0:T(8,128)(2,1)} async-done(((bf16[16,56,2432]{2,1,0:T(8,128)(2,1)}), bf16[16,56,2432]{2,1,0:T(8,128)(2,1)}, u32[]{:S(2)}, u32[]{:S(2)}) %all-to-all-start) | async-done | bytes 4358176 | tf_op jit(solution)/shard_map/all_to_all | solution.py:64
  177.5 5.1 %conditional.2 = (bf16[896,2432]{0,1:T(8,128)(2,1)}) conditional(s32[]{:T(128)} %clamp.4, (bf16[896,2432]{1,0:T(8,128)(2,1)}, bf16[896,896]{1,0:T(8,128)(2,1)}) %tuple.144, (bf16[896,2432]{1,0:T(8,128)(2,1)}, bf16[896,896]{1,0:T(8,128)(2,1)}) %tuple.145, (bf16[896,896]{1,0:T(8,128)(2,1)}, bf16[896,2432]{1,0:T(8,128)(2,1)}) %tuple.146), branch_computations={%region_9.0_spmd, %region_10.0_spmd, %region_11.0_spmd} | conditional | flops 3904897024 | bytes 10321928 | solution.py:97
  177.5 2.8 fusion
  180.3 2.3 pad.10
  182.7 7.1 %copy.72 = bf16[896,2432]{1,0:T(8,128)(2,1)} copy(bf16[896,2432]{0,1:T(8,128)(2,1)} %get-tuple-element.397) | data formatting | bytes 8716288 | tf_op jit(solution)/shard_map/cond | solution.py:97
  189.8 25.4 %all-to-all-start.1 = ((bf16[16,56,2432]{2,1,0:T(8,128)(2,1)}), bf16[16,56,2432]{2,1,0:T(8,128)(2,1)}, u32[]{:S(2)}, u32[]{:S(2)}) async-start(bf16[16,56,2432]{2,1,0:T(8,128)(2,1)} %bitcast.96), calls=%async_computation.1 | async-start | bytes 8716288 | tf_op jit(solution)/shard_map/all_to_all | solution.py:101
  215.2 4.5 %conditional.3 = (f32[896,896]{1,0:T(8,128)}) conditional(s32[]{:T(128)} %clamp.4, bf16[896,2432]{1,0:T(8,128)(2,1)} %bitcast.1, bf16[896,2432]{1,0:T(8,128)(2,1)} %bitcast.1, bf16[896,2432]{1,0:T(8,128)(2,1)} %bitcast.1), branch_computations={%region_28.29_spmd, %region_29.30_spmd, %region_30.31_spmd} | conditional | flops 3904897024 | bytes 7569416 | solution.py:83
  215.4 4.4 %fusion.4 = f32[896,896]{1,0:T(8,128)} fusion(bf16[896,2432]{1,0:T(8,128)(2,1)} %param.3), kind=kOutput, calls=%fused_computation.14 | convolution fusion | flops 719323136 | bytes 4128768 | tf_op jit(solution)/shard_map/cond/branch_0_fun/dot_general | solution.py:35
  219.8 1.5 copy-done.1
  221.3 20.8 %divide_multiply_fusion = (f32[2,56,1,8320]{3,2,1,0:T(1,128)S(1)}, f32[2,56,1,8320]{3,2,1,0:T(1,128)}, f32[2,56,1,8320]{3,2,1,0:T(1,128)}) fusion(bf16[2,56,1,8320]{3,1,2,0:T(8,128)(2,1)S(1)} %copy-done.1, f32[2,56,1,8320]{3,2,1,0:T(1,128)} %param.22, f32[2,56,1,8320]{3,2,1,0:T(1,128)} %param.21), kind=kLoop, calls=%fused_computation.36 | loop fusion | flops 10250240 | bytes 20500480 | tf_op jit(solution)/shard_map/mul | solution.py:57
  242.5 1.8 copy-done
  244.7 1.2 slice_reduce_fusion.8
  246.1 2.2 slice_reduce_fusion.3
  249.4 3.4 fusion.10
  252.7 43.8 %all-to-all-done.1 = bf16[16,56,2432]{2,1,0:T(8,128)(2,1)} async-done(((bf16[16,56,2432]{2,1,0:T(8,128)(2,1)}), bf16[16,56,2432]{2,1,0:T(8,128)(2,1)}, u32[]{:S(2)}, u32[]{:S(2)}) %all-to-all-start.1) | async-done | bytes 4358176 | tf_op jit(solution)/shard_map/all_to_all | solution.py:101
  296.5 12.8 %copy.73 = bf16[16,56,2432]{1,0,2:T(8,128)(2,1)} copy(bf16[16,56,2432]{2,1,0:T(8,128)(2,1)} %all-to-all-done.1) | data formatting | bytes 8716288 | tf_op jit(solution)/shard_map/all_to_all | solution.py:101
  309.3 1.8 gather_fusion.2
  311.8 1.8 gather_fusion.1
  314.3 3.1 gather_fusion.3
  317.4 2.9 gather_fusion
  321.9 2.9 gather_fusion.4
  324.7 2.9 gather_fusion.5
  327.6 2.9 gather_fusion.6
  330.5 2.8 concatenate.57
  337.4 55.1 %all-reduce.6 = (f32[2,7]{1,0:T(2,128)S(1)}, f32[2,7]{1,0:T(2,128)S(1)}) all-reduce(f32[2,7]{1,0:T(2,128)S(1)} %stack.63, f32[2,7]{1,0:T(2,128)S(1)} %stack.55), channel_id=1, replica_groups=mesh['fsdp'=16,'tp'=2] {'fsdp','tp'}, use_global_device_ids=true, to_apply=%region_27.28 | all-reduce | flops 28 | bytes 224 | tf_op jit(solution)/shard_map/psum | solution.py:107
  392.8 2.8 concatenate.56
  396.2 2.6 copy_subtract_fusion
  398.8 5.7 %copy.101 = f32[2,56,1,8320]{3,2,1,0:T(1,128)} copy(f32[2,56,1,8320]{3,1,0,2:T(8,128)S(1)} %copy_subtract_fusion) | data formatting | bytes 7454720
  (104 shorter events, 17.7 us)
Async XLA Ops:
  7.2 3.5 copy-start.9
  9.1 4.2 %copy-start.10 = (s32[3]{0:T(128)S(1)}, s32[3]{0:T(128)}, u32[]{:S(2)}) copy-start(s32[3]{0:T(128)} %constant.291) | copy-start | bytes 40
  10.6 19.5 %copy-start.11 = (s32[3]{0:T(128)S(1)}, s32[3]{0:T(128)}, u32[]{:S(2)}) copy-start(s32[3]{0:T(128)} %constant.305) | copy-start | bytes 40
  86.3 9.9 %copy-start.15 = (s32[7]{0:T(128)S(1)}, s32[7]{0:T(128)}, u32[]{:S(2)}) copy-start(s32[7]{0:T(128)} %constant.14.clone) | copy-start | bytes 88
  86.3 91.2 %all-to-all-start = ((bf16[16,56,2432]{2,1,0:T(8,128)(2,1)}), bf16[16,56,2432]{2,1,0:T(8,128)(2,1)}, u32[]{:S(2)}, u32[]{:S(2)}) async-start(bf16[16,56,2432]{2,1,0:T(8,128)(2,1)} %scatter_fusion.2), calls=%async_computation | async-start | bytes 8716288 | tf_op jit(solution)/shard_map/all_to_all | solution.py:64
  94.8 13.5 %all-gather.3.cloned.1.call-start = ((), (), s32[]{:S(2)}) async-start(), calls=%async_computation.4 | async-start | bytes 2408448 | tf_op jit(solution)/shard_map/all_gather | solution.py:99
  189.8 106.8 %all-to-all-start.1 = ((bf16[16,56,2432]{2,1,0:T(8,128)(2,1)}), bf16[16,56,2432]{2,1,0:T(8,128)(2,1)}, u32[]{:S(2)}, u32[]{:S(2)}) async-start(bf16[16,56,2432]{2,1,0:T(8,128)(2,1)} %bitcast.96), calls=%async_computation.1 | async-start | bytes 8716288 | tf_op jit(solution)/shard_map/all_to_all | solution.py:101
  215.2 34.2 %reduce-scatter.2.cloned.1.call-start = ((), (), s32[]{:S(2)}) async-start(), calls=%async_computation.3 | async-start | bytes 4816896 | tf_op jit(solution)/shard_map/reduce_scatter | solution.py:85
  219.8 1.5 copy-start.1
  242.4 1.9 copy-start
  242.4 6.3 %copy-start.12 = (f32[2,92]{1,0:T(2,128)S(1)}, f32[2,92]{1,0:T(2,128)}, u32[]{:S(2)}) copy-start(f32[2,92]{1,0:T(2,128)} %param.25) | copy-start | bytes 2212
  242.4 6.3 %copy-start.13 = (f32[2,92]{1,0:T(2,128)S(1)}, f32[2,92]{1,0:T(2,128)}, u32[]{:S(2)}) copy-start(f32[2,92]{1,0:T(2,128)} %param.27) | copy-start | bytes 2212
  242.4 6.3 %copy-start.14 = (f32[2,92]{1,0:T(2,128)S(1)}, f32[2,92]{1,0:T(2,128)}, u32[]{:S(2)}) copy-start(f32[2,92]{1,0:T(2,128)} %param.28) | copy-start | bytes 2212
  242.4 6.3 %copy-start.16 = (bf16[2,92]{1,0:T(2,128)(2,1)S(1)}, bf16[2,92]{1,0:T(2,128)(2,1)}, u32[]{:S(2)}) copy-start(bf16[2,92]{1,0:T(2,128)(2,1)} %param.26) | copy-start | bytes 1108
  242.5 6.9 %copy-start.2 = (f32[1,448,896]{2,1,0:T(8,128)S(1)}, f32[1,448,896]{2,1,0:T(8,128)}, u32[]{:S(2)}) copy-start(f32[1,448,896]{2,1,0:T(8,128)} %param.23) | copy-start | bytes 4816900
  313.6 3.8 copy-start.7
  317.4 10.2 %copy-start.5 = (bf16[2,56,448]{1,0,2:T(2,128)(2,1)}, bf16[2,56,448]{1,0,2:T(2,128)(2,1)S(1)}, u32[]{:S(2)}) copy-start(bf16[2,56,448]{1,0,2:T(2,128)(2,1)S(1)} %gather_fusion.3) | copy-start | bytes 301060
  320.3 7.3 %copy-start.3 = (bf16[2,56,448]{1,0,2:T(2,128)(2,1)}, bf16[2,56,448]{1,0,2:T(2,128)(2,1)S(1)}, u32[]{:S(2)}) copy-start(bf16[2,56,448]{1,0,2:T(2,128)(2,1)S(1)} %gather_fusion) | copy-start | bytes 301060
  333.6 1.5 copy-start.8
  333.6 1.6 copy-start.6
  333.6 3.1 copy-start.4
Sparse Core Ops, SparseCore 0:
  97.2 11.0 all-gather.2
  219.9 17.0 reduce-scatter.1
where the time goes:
time: 415 us; the launch traced here: 411 us
  waiting for transfers between devices  124 us (30%)
  local copies, waits for them, and re-layouts  103 us (25%)
  other arithmetic  72.3 us (17%)
  blocking collectives  55.1 us (13%)
  starting transfers between devices  34 us (8%)
  between operations  15.6 us (4%)
  matrix products  7.14 us (2%)
    all_to_all x1, waiting for transfers between devices, on_device(): lax.all_to_all(outgoing, 'fsdp', split_axis=0, concat_axis=0, tiled=True)  69.2 us
    psum x1, blocking collectives, on_device(): shampoo_total = lax.psum(shampoo_part, ('fsdp', 'tp'))  55.1 us
    all_to_all x1, waiting for transfers between devices, on_device(): lax.all_to_all(precond.reshape(chips, rows, capacity), 'fsdp', split_axis...  43.8 us
    scatter x16, other arithmetic  38.8 us
    scatter x24, local copies, waits for them, and re-layouts  26.9 us
    all_to_all x1, starting transfers between devices, on_device(): lax.all_to_all(precond.reshape(chips, rows, capacity), 'fsdp', split_axis...  25.4 us
    gather x11, local copies, waits for them, and re-layouts, on_device(): pieces = [returned[owner[:, kind], :, :widths[kind]] for kind in range(7)]  21.1 us
    mul x1, other arithmetic, on_device(): adam_part = kind_sums(adam_step * adam_step, widths, starts)  20.8 us
  transfers between devices with their start and end apart: 4, of which 3 were waited for; matrix products, arithmetic and copies ran while one was open for 9% of the time, Pallas kernels for 0%

commit v1 on v0

--- a/solution.py
+++ b/solution.py
@@ -104,7 +104,7 @@
     pieces = [returned[owner[:, kind], :, : widths[kind]] for kind in range(7)]
     direction = jnp.concatenate(pieces, axis=2).astype(jnp.float32)
     shampoo_part = kind_sums(direction * direction, widths, starts)
-    shampoo_total = lax.psum(shampoo_part, ("fsdp", "tp"))
+    shampoo_total = lax.psum(lax.psum(shampoo_part, "tp"), "fsdp")
     ratio = jnp.sqrt(adam_total) / (jnp.sqrt(shampoo_total) + 1e-06)
     column_scale = jnp.concatenate(
         [jnp.broadcast_to(ratio[:, kind : kind + 1], (layers, widths[kind])) for kind in range(7)],

time: 415 us -> 442 us (1.065)
  blocking collectives: 55.1 us -> 127 us
  waiting for transfers between devices: 124 us -> 80.2 us
    psum x1 -> x3, blocking collectives: 55.1 us -> 127 us  [the longest x1 82.8 us: on_device(): adam_total = lax.psum(adam_part, ('fsdp', 'tp'))]
    all_to_all x1, waiting for transfers between devices: 43.8 us -> 0.01 us  [on_device(): lax.all_to_all(precond.reshape(chips, rows, capacity), 'fsdp', split_axis...]
  transfers between devices with their start and end apart: 4 -> 4, of which waited for: 3 -> 2; matrix products, arithmetic and copies ran while one was open for 9% -> 8% of each run, Pallas kernels for 0% -> 0%
where the time goes in v1:
time: 442 us; the launch traced here: 439 us
  blocking collectives  127 us (29%)
  local copies, waits for them, and re-layouts  103 us (23%)
  waiting for transfers between devices  80.2 us (18%)
  other arithmetic  72.3 us (16%)
  starting transfers between devices  34 us (8%)
  between operations  15.6 us (4%)
  matrix products  7.14 us (2%)
    psum x1, blocking collectives, on_device(): adam_total = lax.psum(adam_part, ('fsdp', 'tp'))  82.8 us
    all_to_all x1, waiting for transfers between devices, on_device(): lax.all_to_all(outgoing, 'fsdp', split_axis=0, concat_axis=0, tiled=True)  69.2 us
    psum x2, blocking collectives, on_device(): shampoo_total = lax.psum(lax.psum(shampoo_part, 'tp'), 'fsdp')  43.8 us
    scatter x16, other arithmetic  38.8 us
    scatter x24, local copies, waits for them, and re-layouts  26.9 us
    all_to_all x1, starting transfers between devices, on_device(): lax.all_to_all(precond.reshape(chips, rows, capacity), 'fsdp', split_axis...  25.4 us
    gather x11, local copies, waits for them, and re-layouts, on_device(): pieces = [returned[owner[:, kind], :, :widths[kind]] for kind in range(7)]  21.1 us
    mul x1, other arithmetic, on_device(): adam_part = kind_sums(adam_step * adam_step, widths, starts)  20.8 us
  transfers between devices with their start and end apart: 4, of which 2 were waited for; matrix products, arithmetic and copies ran while one was open for 8% of the time, Pallas kernels for 0%

profile of v1, /device:TPU:0, one launch (start us, length us, event | category | flops | bytes accessed | tf_op | source)
XLA Modules:
  0.0 439.1 jit_solution(17917410794300768460)
XLA Ops:
  9.1 1.5 fusion.24
  11.0 2.3 broadcast_in_dim.46
  13.3 16.8 %while.4 = (s32[]{:T(128)}, bf16[16,56,2432]{2,1,0:T(8,128)(2,1)}, s32[2,2]{1,0:T(2,128)S(1)}, bf16[2,56,448]{2,1,0:T(8,128)(2,1)S(1)}, s32[]{:T(128)}, /*index=5*/s32[3]{0:T(128)S(1)}, s32[1]{0:T(128)}, s32[]{:T(128)}) while((s32[]{:T(128)}, bf16[16,56,2432]{2,1,0:T(8,128)(2,1)}, s32[2,2]{1,0:T(2,128)S(1)}, bf16[2,56,448]{2,1,0:T(8,128)(2,1)S(1)}, ...), condition=%wide.while_cond, body=%wide.while_body.sunk | while | flops 25107 | bytes 251051 | solution.py:61
  13.9 2.0 and_reduce_fusion.8
  15.9 2.9 dynamic-slice_select_fusion.8
  18.8 2.9 dynamic-update-slice.12
  22.3 2.0 and_reduce_fusion.8
  24.3 2.9 dynamic-slice_select_fusion.8
  27.2 2.9 dynamic-update-slice.12
  30.1 16.1 %while.5 = (s32[]{:T(128)}, bf16[16,56,2432]{2,1,0:T(8,128)(2,1)}, s32[2,2]{1,0:T(2,128)S(1)}, bf16[2,56,64]{2,1,0:T(8,128)(2,1)S(1)}, s32[]{:T(128)}, /*index=5*/s32[3]{0:T(128)S(1)}, s32[1]{0:T(128)}, s32[]{:T(128)}) while((s32[]{:T(128)}, bf16[16,56,2432]{2,1,0:T(8,128)(2,1)}, s32[2,2]{1,0:T(2,128)S(1)}, bf16[2,56,64]{2,1,0:T(8,128)(2,1)S(1)}, ...), condition=%wide.while_cond.1, body=%wide.while_body.1.sunk | while | flops 3603 | bytes 36011 | solution.py:61
  30.7 2.0 and_reduce_fusion.9
  32.7 2.8 dynamic-slice_select_fusion.9
  35.5 2.7 dynamic-update-slice.13
  38.7 2.0 and_reduce_fusion.9
  40.7 2.8 dynamic-slice_select_fusion.9
  43.5 2.7 dynamic-update-slice.13
  46.2 16.1 %while.6 = (s32[]{:T(128)}, bf16[16,56,2432]{2,1,0:T(8,128)(2,1)}, s32[2,2]{1,0:T(2,128)S(1)}, bf16[2,56,64]{2,1,0:T(8,128)(2,1)S(1)}, s32[]{:T(128)}, /*index=5*/s32[3]{0:T(128)S(1)}, s32[1]{0:T(128)}, s32[]{:T(128)}) while((s32[]{:T(128)}, bf16[16,56,2432]{2,1,0:T(8,128)(2,1)}, s32[2,2]{1,0:T(2,128)S(1)}, bf16[2,56,64]{2,1,0:T(8,128)(2,1)S(1)}, ...), condition=%wide.while_cond.2, body=%wide.while_body.2.sunk | while | flops 3603 | bytes 36011 | solution.py:61
  46.8 2.0 and_reduce_fusion.10
  48.8 2.8 dynamic-slice_select_fusion.10
  51.5 2.7 dynamic-update-slice.14
  54.8 2.0 and_reduce_fusion.10
  56.8 2.8 dynamic-slice_select_fusion.10
  59.6 2.7 dynamic-update-slice.14
  62.3 16.7 %while.7 = (s32[]{:T(128)}, bf16[16,56,2432]{2,1,0:T(8,128)(2,1)}, s32[2,2]{1,0:T(2,128)S(1)}, bf16[2,56,448]{2,1,0:T(8,128)(2,1)S(1)}, s32[]{:T(128)}, /*index=5*/s32[3]{0:T(128)S(1)}, s32[1]{0:T(128)}, s32[]{:T(128)}) while((s32[]{:T(128)}, bf16[16,56,2432]{2,1,0:T(8,128)(2,1)}, s32[2,2]{1,0:T(2,128)S(1)}, bf16[2,56,448]{2,1,0:T(8,128)(2,1)S(1)}, ...), condition=%wide.while_cond.3, body=%wide.while_body.3.sunk | while | flops 25107 | bytes 251051 | solution.py:61
  62.9 2.0 and_reduce_fusion.11
  64.9 2.9 dynamic-slice_select_fusion.11
  67.8 2.9 dynamic-update-slice.15
  71.2 2.0 and_reduce_fusion.11
  73.2 2.9 dynamic-slice_select_fusion.11
  76.2 2.9 dynamic-update-slice.15
  79.0 2.4 scatter_fusion
  81.5 2.4 scatter_fusion.1
  83.9 2.4 scatter_fusion.2
  86.3 8.5 %all-to-all-start = ((bf16[16,56,2432]{2,1,0:T(8,128)(2,1)}), bf16[16,56,2432]{2,1,0:T(8,128)(2,1)}, u32[]{:S(2)}, u32[]{:S(2)}) async-start(bf16[16,56,2432]{2,1,0:T(8,128)(2,1)} %scatter_fusion.2), calls=%async_computation | async-start | bytes 8716288 | tf_op jit(solution)/shard_map/all_to_all | solution.py:64
  98.0 10.3 %all-gather.3.cloned.1.call-done = bf16[1,896,896]{2,1,0:T(8,128)(2,1)} async-done(((bf16[1,448,896]{2,1,0:T(8,128)(2,1)}), bf16[1,896,896]{2,1,0:T(8,128)(2,1)}) %all-gather.3.cloned.1.call-update) | async-done | bytes 1605648 | tf_op jit(solution)/shard_map/all_gather | solution.py:99
  108.3 69.2 %all-to-all-done = bf16[16,56,2432]{2,1,0:T(8,128)(2,1)} async-done(((bf16[16,56,2432]{2,1,0:T(8,128)(2,1)}), bf16[16,56,2432]{2,1,0:T(8,128)(2,1)}, u32[]{:S(2)}, u32[]{:S(2)}) %all-to-all-start) | async-done | bytes 4358176 | tf_op jit(solution)/shard_map/all_to_all | solution.py:64
  177.5 5.1 %conditional.2 = (bf16[896,2432]{0,1:T(8,128)(2,1)}) conditional(s32[]{:T(128)} %clamp.4, (bf16[896,2432]{1,0:T(8,128)(2,1)}, bf16[896,896]{1,0:T(8,128)(2,1)}) %tuple.144, (bf16[896,2432]{1,0:T(8,128)(2,1)}, bf16[896,896]{1,0:T(8,128)(2,1)}) %tuple.145, (bf16[896,896]{1,0:T(8,128)(2,1)}, bf16[896,2432]{1,0:T(8,128)(2,1)}) %tuple.146), branch_computations={%region_9.0_spmd, %region_10.0_spmd, %region_11.0_spmd} | conditional | flops 3904897024 | bytes 10321928 | solution.py:97
  177.5 2.8 fusion
  180.3 2.3 pad.10
  182.7 7.1 %copy.72 = bf16[896,2432]{1,0:T(8,128)(2,1)} copy(bf16[896,2432]{0,1:T(8,128)(2,1)} %get-tuple-element.395) | data formatting | bytes 8716288 | tf_op jit(solution)/shard_map/cond | solution.py:97
  189.8 25.4 %all-to-all-start.1 = ((bf16[16,56,2432]{2,1,0:T(8,128)(2,1)}), bf16[16,56,2432]{2,1,0:T(8,128)(2,1)}, u32[]{:S(2)}, u32[]{:S(2)}) async-start(bf16[16,56,2432]{2,1,0:T(8,128)(2,1)} %bitcast.96), calls=%async_computation.1 | async-start | bytes 8716288 | tf_op jit(solution)/shard_map/all_to_all | solution.py:101
  215.2 4.5 %conditional.3 = (f32[896,896]{1,0:T(8,128)}) conditional(s32[]{:T(128)} %clamp.4, bf16[896,2432]{1,0:T(8,128)(2,1)} %bitcast.1, bf16[896,2432]{1,0:T(8,128)(2,1)} %bitcast.1, bf16[896,2432]{1,0:T(8,128)(2,1)} %bitcast.1), branch_computations={%region_29.30_spmd, %region_30.31_spmd, %region_31.32_spmd} | conditional | flops 3904897024 | bytes 7569416 | solution.py:83
  215.4 4.4 fusion.4
  219.8 1.5 copy-done.1
  221.3 20.8 %divide_multiply_fusion = (f32[2,56,1,8320]{3,2,1,0:T(1,128)S(1)}, f32[2,56,1,8320]{3,2,1,0:T(1,128)}, f32[2,56,1,8320]{3,2,1,0:T(1,128)}) fusion(bf16[2,56,1,8320]{3,1,2,0:T(8,128)(2,1)S(1)} %copy-done.1, f32[2,56,1,8320]{3,2,1,0:T(1,128)} %param.22, f32[2,56,1,8320]{3,2,1,0:T(1,128)} %param.21), kind=kLoop, calls=%fused_computation.36 | loop fusion | flops 10250240 | bytes 20500480 | tf_op jit(solution)/shard_map/mul | solution.py:57
  242.5 1.8 copy-done
  244.7 1.2 slice_reduce_fusion.8
  246.1 2.2 slice_reduce_fusion.3
  248.7 82.8 %psum.21 = f32[2,7]{1,0:T(2,128)S(1)} all-reduce(f32[2,7]{1,0:T(2,128)S(1)} %stack.55), channel_id=1, replica_groups=mesh['fsdp'=16,'tp'=2] {'fsdp','tp'}, use_global_device_ids=true, to_apply=%region_19.20 | all-reduce | flops 14 | bytes 112 | tf_op jit(solution)/shard_map/psum | solution.py:58
  332.2 3.4 fusion.10
  335.6 12.8 %copy.73 = bf16[16,56,2432]{1,0,2:T(8,128)(2,1)} copy(bf16[16,56,2432]{2,1,0:T(8,128)(2,1)} %all-to-all-done.1) | data formatting | bytes 8716288 | tf_op jit(solution)/shard_map/all_to_all | solution.py:101
  348.4 1.8 gather_fusion.2
  350.8 1.8 gather_fusion.1
  353.3 3.1 gather_fusion.3
  356.4 2.9 gather_fusion
  360.9 2.9 gather_fusion.4
  363.7 2.9 gather_fusion.5
  366.6 2.9 gather_fusion.6
  369.5 2.8 concatenate.57
  376.5 2.4 psum.22
  378.9 41.3 %psum.23 = f32[2,7]{1,0:T(2,128)S(1)} all-reduce(f32[2,7]{1,0:T(2,128)S(1)} %psum.22), channel_id=1, replica_groups=mesh['fsdp'=16,'tp'=2] {'fsdp'}, use_global_device_ids=true, to_apply=%region_28.29 | all-reduce | flops 14 | bytes 112 | tf_op jit(solution)/shard_map/psum | solution.py:107
  420.6 2.8 concatenate.56
  424.0 2.6 copy_subtract_fusion
  426.5 5.7 %copy.101 = f32[2,56,1,8320]{3,2,1,0:T(1,128)} copy(f32[2,56,1,8320]{3,1,0,2:T(8,128)S(1)} %copy_subtract_fusion) | data formatting | bytes 7454720
  (106 shorter events, 18.8 us)
Async XLA Ops:
  7.2 3.5 copy-start.9
  9.1 4.2 copy-start.10
  10.6 19.5 %copy-start.11 = (s32[3]{0:T(128)S(1)}, s32[3]{0:T(128)}, u32[]{:S(2)}) copy-start(s32[3]{0:T(128)} %constant.305) | copy-start | bytes 40
  86.3 9.9 %copy-start.15 = (s32[7]{0:T(128)S(1)}, s32[7]{0:T(128)}, u32[]{:S(2)}) copy-start(s32[7]{0:T(128)} %constant.14.clone) | copy-start | bytes 88
  86.3 91.2 %all-to-all-start = ((bf16[16,56,2432]{2,1,0:T(8,128)(2,1)}), bf16[16,56,2432]{2,1,0:T(8,128)(2,1)}, u32[]{:S(2)}, u32[]{:S(2)}) async-start(bf16[16,56,2432]{2,1,0:T(8,128)(2,1)} %scatter_fusion.2), calls=%async_computation | async-start | bytes 8716288 | tf_op jit(solution)/shard_map/all_to_all | solution.py:64
  94.8 13.5 %all-gather.3.cloned.1.call-start = ((), (), s32[]{:S(2)}) async-start(), calls=%async_computation.4 | async-start | bytes 2408448 | tf_op jit(solution)/shard_map/all_gather | solution.py:99
  189.8 145.8 %all-to-all-start.1 = ((bf16[16,56,2432]{2,1,0:T(8,128)(2,1)}), bf16[16,56,2432]{2,1,0:T(8,128)(2,1)}, u32[]{:S(2)}, u32[]{:S(2)}) async-start(bf16[16,56,2432]{2,1,0:T(8,128)(2,1)} %bitcast.96), calls=%async_computation.1 | async-start | bytes 8716288 | tf_op jit(solution)/shard_map/all_to_all | solution.py:101
  215.2 117.0 %reduce-scatter.2.cloned.1.call-start = ((), (), s32[]{:S(2)}) async-start(), calls=%async_computation.3 | async-start | bytes 4816896 | tf_op jit(solution)/shard_map/reduce_scatter | solution.py:85
  219.8 1.5 copy-start.1
  242.4 1.9 copy-start
  242.4 89.2 %copy-start.12 = (f32[2,92]{1,0:T(2,128)S(1)}, f32[2,92]{1,0:T(2,128)}, u32[]{:S(2)}) copy-start(f32[2,92]{1,0:T(2,128)} %param.25) | copy-start | bytes 2212
  242.4 89.2 %copy-start.13 = (f32[2,92]{1,0:T(2,128)S(1)}, f32[2,92]{1,0:T(2,128)}, u32[]{:S(2)}) copy-start(f32[2,92]{1,0:T(2,128)} %param.27) | copy-start | bytes 2212
  242.4 89.2 %copy-start.14 = (f32[2,92]{1,0:T(2,128)S(1)}, f32[2,92]{1,0:T(2,128)}, u32[]{:S(2)}) copy-start(f32[2,92]{1,0:T(2,128)} %param.28) | copy-start | bytes 2212
  242.4 89.2 %copy-start.16 = (bf16[2,92]{1,0:T(2,128)(2,1)S(1)}, bf16[2,92]{1,0:T(2,128)(2,1)}, u32[]{:S(2)}) copy-start(bf16[2,92]{1,0:T(2,128)(2,1)} %param.26) | copy-start | bytes 1108
  242.5 89.7 %copy-start.2 = (f32[1,448,896]{2,1,0:T(8,128)S(1)}, f32[1,448,896]{2,1,0:T(8,128)}, u32[]{:S(2)}) copy-start(f32[1,448,896]{2,1,0:T(8,128)} %param.23) | copy-start | bytes 4816900
  352.6 0.7 copy-start.7
  356.4 10.2 %copy-start.3 = (bf16[2,56,448]{1,0,2:T(2,128)(2,1)}, bf16[2,56,448]{1,0,2:T(2,128)(2,1)S(1)}, u32[]{:S(2)}) copy-start(bf16[2,56,448]{1,0,2:T(2,128)(2,1)S(1)} %gather_fusion.3) | copy-start | bytes 301060
  359.3 7.3 %copy-start.5 = (bf16[2,56,448]{1,0,2:T(2,128)(2,1)}, bf16[2,56,448]{1,0,2:T(2,128)(2,1)S(1)}, u32[]{:S(2)}) copy-start(bf16[2,56,448]{1,0,2:T(2,128)(2,1)S(1)} %gather_fusion) | copy-start | bytes 301060
  372.6 1.5 copy-start.8
  372.6 1.6 copy-start.4
  372.6 2.3 copy-start.6
Sparse Core Ops, SparseCore 0:
  97.2 11.0 all-gather.2
  219.9 17.0 reduce-scatter.1
